TPU v7x, 32 devices: a whole 2x2x4 slice. The times are simulated.
32 devices in a mesh: slab: 2 (over y), tile: 4 (over z), view: 4 (over x, core).
Axes of the slice: x: 2, y: 2, z: 4, core: 2. Of those that a mesh axis runs over, the one named last changes fastest.
Arguments:
- recorded: float32 [4, 96, 32, 1024], P('view', 'tile', 'slab'), parts along dimension 2, may hold values from 0.5 to 2
- psf_taps: float32 [4, 3, 15], P('view'), may hold values from 0.2 to 1
- estimate: float32 [96, 32, 1024], P('tile', 'slab'), parts along dimension 1, may hold values from 0.5 to 2
Outputs:
- joined: float32 [96, 32, 1024], P('tile', 'slab'), parts along dimension 1
There are 2 independent parts, one for each index of `slab`. A program takes and returns all parts, laid end to end along the dimension named above; an argument that names none is the same for every part. Nothing has to cross between parts.
All inputs are finite; a program needn't handle non-finite values.
Results may differ from a plain program's by a relative error of at most 0.00002.
Values sent between devices are 32-bit elements; how exact they have to be, the bound alone decides.
No kernel may reach another device: no remote copies, remote signals or barrier semaphores. Data moves between devices by JAX's collectives and lax.ppermute only.
A program may use at most 64 MiB of HBM per device.

v0:
```python
import jax
import jax.numpy as jnp
from jax import lax
from jax.sharding import PartitionSpec as P

RADIUS = 7
ITERS = 2


def with_halo(shard, sides, width):
    for axis, dim in sides:
        devices, length = (lax.axis_size(axis), shard.shape[dim])
        up = [(i, (i + 1) % devices) for i in range(devices - 1)]
        down = [(j, i) for i, j in up]
        last = lax.slice_in_dim(shard, length - width, length, axis=dim)
        initial = lax.slice_in_dim(shard, 0, width, axis=dim)
        before = lax.ppermute(last, axis, up)
        after = lax.ppermute(initial, axis, down)
        shard = jnp.concatenate([before, shard, after], axis=dim)
    return shard


def valid_along(padded, kernel_row, axis_num, mirrored):
    length_out = padded.shape[axis_num] - 2 * RADIUS
    summed = jnp.zeros(
        padded.shape[:axis_num] + (length_out,) + padded.shape[axis_num + 1 :], jnp.float32
    )
    for offset in range(2 * RADIUS + 1):
        weight = kernel_row[2 * RADIUS - offset] if mirrored else kernel_row[offset]
        summed = summed + weight * lax.slice_in_dim(
            padded, offset, offset + length_out, axis=axis_num
        )
    return summed


def along(values_in, kernel_row, axis_num, mirrored):
    widths = [(0, 0)] * values_in.ndim
    widths[axis_num] = (RADIUS, RADIUS)
    return valid_along(jnp.pad(values_in, widths), kernel_row, axis_num, mirrored)


def finish_zy(values_in, kernel_view, mirrored):
    result = along(values_in, kernel_view[1], 1, mirrored)
    return along(result, kernel_view[2], 2, mirrored)


def local(recorded, psf_taps, estimate):
    kernel = psf_taps / jnp.sum(psf_taps, axis=2, keepdims=True)
    local_views = recorded.shape[0]
    view_total = lax.axis_size("view") * local_views
    for iteration in range(ITERS):
        extended = with_halo(estimate, (("tile", 0),), RADIUS)
        kernel_view = kernel[0]
        blurred = finish_zy(valid_along(extended, kernel_view[0], 0, False), kernel_view, False)
        quotient = recorded[0] / blurred
        quotient_wide = with_halo(quotient, (("tile", 0),), RADIUS)
        correction = finish_zy(
            valid_along(quotient_wide, kernel_view[0], 0, True), kernel_view, True
        )
        log_terms = jnp.log(correction)
        log_total = lax.psum(log_terms, "view")
        estimate = estimate * jnp.exp(log_total / view_total)
    return estimate


def solution(mesh):
    in_specs = (P("view", "tile", "slab", None), P("view", None, None), P("tile", "slab", None))
    out_specs = P("tile", "slab", None)
    return jax.shard_map(local, mesh=mesh, in_specs=in_specs, out_specs=out_specs, check_vma=False)
```

profile of v0, /device:TPU:0, one launch (start us, length us, event | category | flops | bytes accessed | tf_op | source)
XLA Modules:
  0.0 333.5 jit_solution(3361568924771776846)
XLA Ops:
  6.5 0.0 all-reduce.11.cloned.1.call-start
  6.5 1.3 fusion.365
  7.9 5.0 %collective-permute-start = (f32[7,16,1024]{2,1,0:T(8,128)S(1)}, f32[7,16,1024]{2,1,0:T(8,128)S(1)}, u32[]{:S(2)}, u32[]{:S(2)}) collective-permute-start(f32[7,16,1024]{2,1,0:T(8,128)S(1)} %get-tuple-element.13), channel_id=1, source_target_pairs={{0,4},{4,8},{8,12},{1,5},{5,9},{9,13},{2,6},{6,10},{10,14},{3,7},{... | collective-permute-start | bytes 1376264 | tf_op jit(solution)/shard_map/ppermute | solution.py:17
  12.9 1.3 collective-permute-start.1
  14.2 0.1 reduce_sum.9
  14.3 0.1 broadcast_divide_fusion
  14.4 0.7 fusion.367
  15.1 0.6 fusion.368
  15.7 0.7 fusion.366
  16.5 6.1 %collective-permute-done = f32[7,16,1024]{2,1,0:T(8,128)S(1)} collective-permute-done((f32[7,16,1024]{2,1,0:T(8,128)S(1)}, f32[7,16,1024]{2,1,0:T(8,128)S(1)}, u32[]{:S(2)}, u32[]{:S(2)}) %collective-permute-start) | collective-permute-done | bytes 458784 | tf_op jit(solution)/shard_map/ppermute | solution.py:17
  22.7 0.4 constant_dynamic-update-slice_fusion
  23.0 3.7 %collective-permute-done.1 = f32[7,16,1024]{2,1,0:T(8,128)S(1)} collective-permute-done((f32[7,16,1024]{2,1,0:T(8,128)S(1)}, f32[7,16,1024]{2,1,0:T(8,128)S(1)}, u32[]{:S(2)}, u32[]{:S(2)}) %collective-permute-start.1) | collective-permute-done | bytes 458784 | tf_op jit(solution)/shard_map/ppermute | solution.py:18
  26.8 12.1 %fusion.346 = f32[24,16,1024]{2,1,0:T(8,128)S(1)} fusion(f32[31,16,1024]{2,1,0:T(8,128)S(1)} %constant_dynamic-update-slice_fusion.2, f32[31,16,1024]{2,1,0:T(8,128)S(1)} %get-tuple-element.11, f32[24,16,1024]{2,1,0:T(8,128)S(1)} %copy-done, f32[]{:T(128)} %bitcast.19, f32[]{:T(128)} %bitcast.18, f32[]{:T(128)} %bitcast.17, f32[]{:T(128)} %bitcast.16, ...), kind=kLoop, calls=%fused_computation.537 | loop fusion | flops 11403264 | bytes 25165884 | tf_op jit(solution)/shard_map/add | solution.py:30
  38.9 0.0 copy-start.1
  38.9 12.4 %fusion.242 = f32[24,16,1024]{2,1,0:T(8,128)S(1)} fusion(f32[24,16,1024]{2,1,0:T(8,128)S(1)} %fusion.346, f32[]{:T(128)} %bitcast.32, f32[]{:T(128)} %bitcast.31, f32[]{:T(128)} %bitcast.30, f32[]{:T(128)} %bitcast.29, f32[]{:T(128)} %bitcast.28, f32[]{:T(128)} %bitcast.27, f32[]{:T(128)} %bitcast.26, f32[]{:T(128)} %bitcast.25, f32[]{:T(128)} %bitcast.24, ...), kind=kLoop, calls=%fused_computation.426 | loop fusion | flops 11403264 | bytes 3145788 | tf_op jit(solution)/shard_map/add | solution.py:30
  51.2 15.3 %fusion.15 = f32[24,16,1024]{2,1,0:T(8,128)S(1)} fusion(f32[24,16,1024]{2,1,0:T(8,128)S(1)} %fusion.242, f32[1,24,16,1024]{3,2,1,0:T(8,128)S(1)} %copy-done.1, f32[]{:T(128)} %bitcast.45, f32[]{:T(128)} %bitcast.44, f32[]{:T(128)} %bitcast.43, f32[]{:T(128)} %bitcast.42, f32[]{:T(128)} %bitcast.41, f32[]{:T(128)} %bitcast.40, f32[]{:T(128)} %bitcast.39, ...), kind=kLoop, calls=%fused_computation.199 | loop fusion | flops 11796480 | bytes 4718652 | tf_op jit(solution)/shard_map/div | solution.py:55
  66.6 0.1 fusion.364
  66.7 1.3 collective-permute-start.3
  68.0 4.8 %collective-permute-start.2 = (f32[7,16,1024]{2,1,0:T(8,128)S(1)}, f32[7,16,1024]{2,1,0:T(8,128)S(1)}, u32[]{:S(2)}, u32[]{:S(2)}) collective-permute-start(f32[7,16,1024]{2,1,0:T(8,128)S(1)} %get-tuple-element.9), channel_id=1, source_target_pairs={{0,4},{4,8},{8,12},{1,5},{5,9},{9,13},{2,6},{6,10},{10,14},{3,7},{... | collective-permute-start | bytes 1376264 | tf_op jit(solution)/shard_map/ppermute | solution.py:17
  72.7 7.0 %collective-permute-done.3 = f32[7,16,1024]{2,1,0:T(8,128)S(1)} collective-permute-done((f32[7,16,1024]{2,1,0:T(8,128)S(1)}, f32[7,16,1024]{2,1,0:T(8,128)S(1)}, u32[]{:S(2)}, u32[]{:S(2)}) %collective-permute-start.3) | collective-permute-done | bytes 458784 | tf_op jit(solution)/shard_map/ppermute | solution.py:18
  79.7 1.2 collective-permute-done.2
  80.9 12.3 %fusion.193 = f32[24,16,1024]{2,1,0:T(8,128)S(1)} fusion(f32[24,16,1024]{2,1,0:T(8,128)S(1)} %fusion.15, f32[7,16,1024]{2,1,0:T(8,128)S(1)} %collective-permute-done.3, f32[7,16,1024]{2,1,0:T(8,128)S(1)} %collective-permute-done.2, f32[]{:T(128)} %bitcast.19, f32[]{:T(128)} %bitcast.18, f32[]{:T(128)} %bitcast.17, f32[]{:T(128)} %bitcast.16, f32[]{:T(128)} %bitcast.15, ...), kind=kLoop, calls=%fused_computation.377 | loop fusion | flops 16908288 | bytes 4063292 | tf_op jit(solution)/shard_map/add | solution.py:30
  93.1 12.2 %fusion.270 = f32[24,16,1024]{2,1,0:T(8,128)S(1)} fusion(f32[24,16,1024]{2,1,0:T(8,128)S(1)} %fusion.193, f32[]{:T(128)} %bitcast.32, f32[]{:T(128)} %bitcast.31, f32[]{:T(128)} %bitcast.30, f32[]{:T(128)} %bitcast.29, f32[]{:T(128)} %bitcast.28, f32[]{:T(128)} %bitcast.27, f32[]{:T(128)} %bitcast.26, f32[]{:T(128)} %bitcast.25, f32[]{:T(128)} %bitcast.24, ...), kind=kLoop, calls=%fused_computation.454 | loop fusion | flops 11403264 | bytes 3145788 | tf_op jit(solution)/shard_map/add | solution.py:30
  105.4 16.2 %fusion.361 = f32[24,16,1024]{2,1,0:T(8,128)} fusion(f32[24,16,1024]{2,1,0:T(8,128)S(1)} %fusion.270, f32[]{:T(128)} %bitcast.45, f32[]{:T(128)} %bitcast.44, f32[]{:T(128)} %bitcast.43, f32[]{:T(128)} %bitcast.42, f32[]{:T(128)} %bitcast.41, f32[]{:T(128)} %bitcast.40, f32[]{:T(128)} %bitcast.39, f32[]{:T(128)} %bitcast.38, f32[]{:T(128)} %bitcast.37, ...), kind=kLoop, calls=%fused_computation.567 | loop fusion | flops 11403264 | bytes 3145788 | tf_op jit(solution)/shard_map/log | solution.py:60
  121.6 0.0 all-reduce.11.cloned.1.call-update
  121.6 0.0 all-reduce.13.cloned.1.call-start
  121.7 45.1 %all-reduce.11.cloned.1.call-done = f32[24,16,1024]{2,1,0:T(8,128)} async-done(((f32[24,16,1024]{2,1,0:T(8,128)}), f32[24,16,1024]{2,1,0:T(8,128)}) %all-reduce.11.cloned.1.call-update) | async-done | bytes 1572880 | tf_op jit(solution)/shard_map/psum | solution.py:61
  166.8 1.7 exponential_multiply_fusion.1
  168.5 0.1 fusion.363
  168.5 1.3 collective-permute-start.5
  169.8 4.6 %collective-permute-start.4 = (f32[7,16,1024]{2,1,0:T(8,128)S(1)}, f32[7,16,1024]{2,1,0:T(8,128)S(1)}, u32[]{:S(2)}, u32[]{:S(2)}) collective-permute-start(f32[7,16,1024]{2,1,0:T(8,128)S(1)} %get-tuple-element.7), channel_id=1, source_target_pairs={{0,4},{4,8},{8,12},{1,5},{5,9},{9,13},{2,6},{6,10},{10,14},{3,7},{... | collective-permute-start | bytes 1376264 | tf_op jit(solution)/shard_map/ppermute | solution.py:17
  174.4 8.2 %collective-permute-done.5 = f32[7,16,1024]{2,1,0:T(8,128)S(1)} collective-permute-done((f32[7,16,1024]{2,1,0:T(8,128)S(1)}, f32[7,16,1024]{2,1,0:T(8,128)S(1)}, u32[]{:S(2)}, u32[]{:S(2)}) %collective-permute-start.5) | collective-permute-done | bytes 458784 | tf_op jit(solution)/shard_map/ppermute | solution.py:18
  182.6 1.2 collective-permute-done.4
  183.8 12.2 %fusion.155 = f32[24,16,1024]{2,1,0:T(8,128)S(1)} fusion(f32[24,16,1024]{2,1,0:T(8,128)S(1)} %exponential_multiply_fusion.1, f32[7,16,1024]{2,1,0:T(8,128)S(1)} %collective-permute-done.5, f32[7,16,1024]{2,1,0:T(8,128)S(1)} %collective-permute-done.4, f32[]{:T(128)} %bitcast.19, f32[]{:T(128)} %bitcast.18, f32[]{:T(128)} %bitcast.17, f32[]{:T(128)} %bitcast.16, ...), kind=kLoop, calls=%fused_computation.339 | loop fusion | flops 16908288 | bytes 4063292 | tf_op jit(solution)/shard_map/add | solution.py:30
  195.9 0.0 copy-start.2
  195.9 12.4 %fusion.298 = f32[24,16,1024]{2,1,0:T(8,128)S(1)} fusion(f32[24,16,1024]{2,1,0:T(8,128)S(1)} %fusion.155, f32[]{:T(128)} %bitcast.32, f32[]{:T(128)} %bitcast.31, f32[]{:T(128)} %bitcast.30, f32[]{:T(128)} %bitcast.29, f32[]{:T(128)} %bitcast.28, f32[]{:T(128)} %bitcast.27, f32[]{:T(128)} %bitcast.26, f32[]{:T(128)} %bitcast.25, f32[]{:T(128)} %bitcast.24, ...), kind=kLoop, calls=%fused_computation.482 | loop fusion | flops 11403264 | bytes 3145788 | tf_op jit(solution)/shard_map/add | solution.py:30
  208.3 15.3 %fusion.72 = f32[24,16,1024]{2,1,0:T(8,128)S(1)} fusion(f32[24,16,1024]{2,1,0:T(8,128)S(1)} %fusion.298, f32[1,24,16,1024]{3,2,1,0:T(8,128)S(1)} %copy-done.2, f32[]{:T(128)} %bitcast.45, f32[]{:T(128)} %bitcast.44, f32[]{:T(128)} %bitcast.43, f32[]{:T(128)} %bitcast.42, f32[]{:T(128)} %bitcast.41, f32[]{:T(128)} %bitcast.40, f32[]{:T(128)} %bitcast.39, ...), kind=kLoop, calls=%fused_computation.256 | loop fusion | flops 11796480 | bytes 4718652 | tf_op jit(solution)/shard_map/div | solution.py:55
  223.7 0.1 fusion.362
  223.7 1.5 collective-permute-start.7
  225.3 5.0 %collective-permute-start.6 = (f32[7,16,1024]{2,1,0:T(8,128)S(1)}, f32[7,16,1024]{2,1,0:T(8,128)S(1)}, u32[]{:S(2)}, u32[]{:S(2)}) collective-permute-start(f32[7,16,1024]{2,1,0:T(8,128)S(1)} %get-tuple-element.5), channel_id=1, source_target_pairs={{0,4},{4,8},{8,12},{1,5},{5,9},{9,13},{2,6},{6,10},{10,14},{3,7},{... | collective-permute-start | bytes 1376264 | tf_op jit(solution)/shard_map/ppermute | solution.py:17
  230.3 7.1 %collective-permute-done.7 = f32[7,16,1024]{2,1,0:T(8,128)S(1)} collective-permute-done((f32[7,16,1024]{2,1,0:T(8,128)S(1)}, f32[7,16,1024]{2,1,0:T(8,128)S(1)}, u32[]{:S(2)}, u32[]{:S(2)}) %collective-permute-start.7) | collective-permute-done | bytes 458784 | tf_op jit(solution)/shard_map/ppermute | solution.py:18
  237.4 1.4 collective-permute-done.6
  238.8 12.2 %fusion.117 = f32[24,16,1024]{2,1,0:T(8,128)S(1)} fusion(f32[24,16,1024]{2,1,0:T(8,128)S(1)} %fusion.72, f32[7,16,1024]{2,1,0:T(8,128)S(1)} %collective-permute-done.7, f32[7,16,1024]{2,1,0:T(8,128)S(1)} %collective-permute-done.6, f32[]{:T(128)} %bitcast.19, f32[]{:T(128)} %bitcast.18, f32[]{:T(128)} %bitcast.17, f32[]{:T(128)} %bitcast.16, f32[]{:T(128)} %bitcast.15, ...), kind=kLoop, calls=%fused_computation.301 | loop fusion | flops 16908288 | bytes 4063292 | tf_op jit(solution)/shard_map/add | solution.py:30
  251.0 12.2 %fusion.326 = f32[24,16,1024]{2,1,0:T(8,128)S(1)} fusion(f32[24,16,1024]{2,1,0:T(8,128)S(1)} %fusion.117, f32[]{:T(128)} %bitcast.32, f32[]{:T(128)} %bitcast.31, f32[]{:T(128)} %bitcast.30, f32[]{:T(128)} %bitcast.29, f32[]{:T(128)} %bitcast.28, f32[]{:T(128)} %bitcast.27, f32[]{:T(128)} %bitcast.26, f32[]{:T(128)} %bitcast.25, f32[]{:T(128)} %bitcast.24, ...), kind=kLoop, calls=%fused_computation.510 | loop fusion | flops 11403264 | bytes 3145788 | tf_op jit(solution)/shard_map/add | solution.py:30
  263.2 16.2 %fusion.360 = f32[24,16,1024]{2,1,0:T(8,128)} fusion(f32[24,16,1024]{2,1,0:T(8,128)S(1)} %fusion.326, f32[]{:T(128)} %bitcast.45, f32[]{:T(128)} %bitcast.44, f32[]{:T(128)} %bitcast.43, f32[]{:T(128)} %bitcast.42, f32[]{:T(128)} %bitcast.41, f32[]{:T(128)} %bitcast.40, f32[]{:T(128)} %bitcast.39, f32[]{:T(128)} %bitcast.38, f32[]{:T(128)} %bitcast.37, ...), kind=kLoop, calls=%fused_computation.566 | loop fusion | flops 11403264 | bytes 3145788 | tf_op jit(solution)/shard_map/log | solution.py:60
  279.4 0.0 all-reduce.13.cloned.1.call-update
  279.4 44.4 %all-reduce.13.cloned.1.call-done = f32[24,16,1024]{2,1,0:T(8,128)} async-done(((f32[24,16,1024]{2,1,0:T(8,128)}), f32[24,16,1024]{2,1,0:T(8,128)}) %all-reduce.13.cloned.1.call-update) | async-done | bytes 1572880 | tf_op jit(solution)/shard_map/psum | solution.py:61
  323.8 2.8 exponential_multiply_fusion
  (8 shorter events, 0.1 us)
Async XLA Ops:
  6.5 16.1 %copy-start = (f32[24,16,1024]{2,1,0:T(8,128)S(1)}, f32[24,16,1024]{2,1,0:T(8,128)}, u32[]{:S(2)}) copy-start(f32[24,16,1024]{2,1,0:T(8,128)} %param.5) | copy-start | bytes 4718596
  6.5 7.7 %copy-start.3 = (f32[1,3,15]{2,0,1:T(1,128)S(1)}, f32[1,3,15]{2,0,1:T(1,128)}, u32[]{:S(2)}) copy-start(f32[1,3,15]{2,0,1:T(1,128)} %param.4) | copy-start | bytes 544
  6.5 160.2 %all-reduce.11.cloned.1.call-start = ((), (), s32[]{:S(2)}) async-start(), calls=%async_computation | async-start | bytes 3145728 | tf_op jit(solution)/shard_map/psum | solution.py:61
  7.9 14.7 %collective-permute-start = (f32[7,16,1024]{2,1,0:T(8,128)S(1)}, f32[7,16,1024]{2,1,0:T(8,128)S(1)}, u32[]{:S(2)}, u32[]{:S(2)}) collective-permute-start(f32[7,16,1024]{2,1,0:T(8,128)S(1)} %get-tuple-element.13), channel_id=1, source_target_pairs={{0,4},{4,8},{8,12},{1,5},{5,9},{9,13},{2,6},{6,10},{10,14},{3,7},{... | collective-permute-start | bytes 1376264 | tf_op jit(solution)/shard_map/ppermute | solution.py:17
  12.9 13.9 %collective-permute-start.1 = (f32[7,16,1024]{2,1,0:T(8,128)S(1)}, f32[7,16,1024]{2,1,0:T(8,128)S(1)}, u32[]{:S(2)}, u32[]{:S(2)}) collective-permute-start(f32[7,16,1024]{2,1,0:T(8,128)S(1)} %get-tuple-element.14), channel_id=1, source_target_pairs={{4,0},{8,4},{12,8},{5,1},{9,5},{13,9},{6,2},{10,6},{14,10},{7,3},{... | collective-permute-start | bytes 1376264 | tf_op jit(solution)/shard_map/ppermute | solution.py:18
  38.9 12.4 %copy-start.1 = (f32[1,24,16,1024]{3,2,1,0:T(8,128)S(1)}, f32[1,24,16,1024]{3,2,1,0:T(8,128)}, u32[]{:S(2)}) copy-start(f32[1,24,16,1024]{3,2,1,0:T(8,128)} %param.3) | copy-start | bytes 4718596
  66.7 13.0 %collective-permute-start.3 = (f32[7,16,1024]{2,1,0:T(8,128)S(1)}, f32[7,16,1024]{2,1,0:T(8,128)S(1)}, u32[]{:S(2)}, u32[]{:S(2)}) collective-permute-start(f32[7,16,1024]{2,1,0:T(8,128)S(1)} %get-tuple-element.10), channel_id=1, source_target_pairs={{4,0},{8,4},{12,8},{5,1},{9,5},{13,9},{6,2},{10,6},{14,10},{7,3},{... | collective-permute-start | bytes 1376264 | tf_op jit(solution)/shard_map/ppermute | solution.py:18
  68.0 12.9 %collective-permute-start.2 = (f32[7,16,1024]{2,1,0:T(8,128)S(1)}, f32[7,16,1024]{2,1,0:T(8,128)S(1)}, u32[]{:S(2)}, u32[]{:S(2)}) collective-permute-start(f32[7,16,1024]{2,1,0:T(8,128)S(1)} %get-tuple-element.9), channel_id=1, source_target_pairs={{0,4},{4,8},{8,12},{1,5},{5,9},{9,13},{2,6},{6,10},{10,14},{3,7},{... | collective-permute-start | bytes 1376264 | tf_op jit(solution)/shard_map/ppermute | solution.py:17
  121.6 202.2 %all-reduce.13.cloned.1.call-start = ((), (), s32[]{:S(2)}) async-start(), calls=%async_computation.1 | async-start | bytes 3145728 | tf_op jit(solution)/shard_map/psum | solution.py:61
  168.5 14.0 %collective-permute-start.5 = (f32[7,16,1024]{2,1,0:T(8,128)S(1)}, f32[7,16,1024]{2,1,0:T(8,128)S(1)}, u32[]{:S(2)}, u32[]{:S(2)}) collective-permute-start(f32[7,16,1024]{2,1,0:T(8,128)S(1)} %get-tuple-element.8), channel_id=1, source_target_pairs={{4,0},{8,4},{12,8},{5,1},{9,5},{13,9},{6,2},{10,6},{14,10},{7,3},{... | collective-permute-start | bytes 1376264 | tf_op jit(solution)/shard_map/ppermute | solution.py:18
  169.8 13.9 %collective-permute-start.4 = (f32[7,16,1024]{2,1,0:T(8,128)S(1)}, f32[7,16,1024]{2,1,0:T(8,128)S(1)}, u32[]{:S(2)}, u32[]{:S(2)}) collective-permute-start(f32[7,16,1024]{2,1,0:T(8,128)S(1)} %get-tuple-element.7), channel_id=1, source_target_pairs={{0,4},{4,8},{8,12},{1,5},{5,9},{9,13},{2,6},{6,10},{10,14},{3,7},{... | collective-permute-start | bytes 1376264 | tf_op jit(solution)/shard_map/ppermute | solution.py:17
  195.9 12.4 %copy-start.2 = (f32[1,24,16,1024]{3,2,1,0:T(8,128)S(1)}, f32[1,24,16,1024]{3,2,1,0:T(8,128)}, u32[]{:S(2)}) copy-start(f32[1,24,16,1024]{3,2,1,0:T(8,128)} %param.3) | copy-start | bytes 4718596
  223.7 13.7 %collective-permute-start.7 = (f32[7,16,1024]{2,1,0:T(8,128)S(1)}, f32[7,16,1024]{2,1,0:T(8,128)S(1)}, u32[]{:S(2)}, u32[]{:S(2)}) collective-permute-start(f32[7,16,1024]{2,1,0:T(8,128)S(1)} %get-tuple-element.6), channel_id=1, source_target_pairs={{4,0},{8,4},{12,8},{5,1},{9,5},{13,9},{6,2},{10,6},{14,10},{7,3},{... | collective-permute-start | bytes 1376264 | tf_op jit(solution)/shard_map/ppermute | solution.py:18
  225.3 13.5 %collective-permute-start.6 = (f32[7,16,1024]{2,1,0:T(8,128)S(1)}, f32[7,16,1024]{2,1,0:T(8,128)S(1)}, u32[]{:S(2)}, u32[]{:S(2)}) collective-permute-start(f32[7,16,1024]{2,1,0:T(8,128)S(1)} %get-tuple-element.5), channel_id=1, source_target_pairs={{0,4},{4,8},{8,12},{1,5},{5,9},{9,13},{2,6},{6,10},{10,14},{3,7},{... | collective-permute-start | bytes 1376264 | tf_op jit(solution)/shard_map/ppermute | solution.py:17
Sparse Core Ops, SparseCore 0:
  121.7 44.9 all-reduce.10
  279.6 44.1 all-reduce.12
where the time goes:
time: 335 us; the launch traced here: 333 us
  other arithmetic  166 us (50%)
  waiting for transfers between devices  125 us (37%)
  starting transfers between devices  24.8 us (7%)
  between operations  13.7 us (4%)
  local copies, waits for them, and re-layouts  4.11 us (1%)
    add x8, other arithmetic, valid_along(): summed + weight * lax.slice_in_dim(padded, offset, offset + length_out, a...  97.8 us
    psum x2, waiting for transfers between devices, local(): log_total = lax.psum(log_terms, 'view')  89.5 us
    log x2, other arithmetic, local(): log_terms = jnp.log(correction)  32.4 us
    div x2, other arithmetic, local(): quotient = recorded[0] / blurred  30.7 us
    ppermute x4, waiting for transfers between devices, with_halo(): after = lax.ppermute(initial, axis, down)  25.9 us
    ppermute x4, starting transfers between devices, with_halo(): before = lax.ppermute(last, axis, up)  19.4 us
    ppermute x4, waiting for transfers between devices, with_halo(): before = lax.ppermute(last, axis, up)  9.9 us
  transfers between devices with their start and end apart: 10, of which 10 were waited for; matrix products, arithmetic and copies ran while one was open for 1% of the time, Pallas kernels for 0%

commit v1 on v0

--- a/solution.py
+++ b/solution.py
@@ -58,7 +58,11 @@
             valid_along(quotient_wide, kernel_view[0], 0, True), kernel_view, True
         )
         log_terms = jnp.log(correction)
-        log_total = lax.psum(log_terms, "view")
+        log_total = log_terms
+        for hop in (1, 2):
+            log_total = log_total + lax.ppermute(
+                log_total, "view", [(dev, dev ^ hop) for dev in range(4)]
+            )
         estimate = estimate * jnp.exp(log_total / view_total)
     return estimate
 

time: 335 us -> 339 us (1.012)
  other arithmetic: 166 us -> 192 us
  between operations: 13.7 us -> 0.29 us
  waiting for transfers between devices: 125 us -> 112 us
  starting transfers between devices: 24.8 us -> 28.7 us
    psum x2 -> x0, waiting for transfers between devices: 89.5 us -> none  [local(): log_total = lax.psum(log_terms, 'view')]
    ppermute x0 -> x4, waiting for transfers between devices: none -> 76.7 us  [local(): lax.ppermute(log_total, 'view', [(dev, dev ^ hop) for dev in range(4)])]
    add x0 -> x2, other arithmetic: none -> 30.1 us  [local(): log_total + lax.ppermute(log_total, 'view', [(dev, dev ^ hop) for dev in...]
  transfers between devices with their start and end apart: 10 -> 12, of which waited for: 10 -> 12; matrix products, arithmetic and copies ran while one was open for 1% -> 1% of each run, Pallas kernels for 0% -> 0%
where the time goes in v1:
time: 339 us; the launch traced here: 337 us
  other arithmetic  192 us (57%)
  waiting for transfers between devices  112 us (33%)
  starting transfers between devices  28.7 us (8%)
  local copies, waits for them, and re-layouts  4.23 us (1%)
    add x8, other arithmetic, valid_along(): summed + weight * lax.slice_in_dim(padded, offset, offset + length_out, a...  99.5 us
    ppermute x4, waiting for transfers between devices, local(): lax.ppermute(log_total, 'view', [(dev, dev ^ hop) for dev in range(4)])  76.7 us
    div x2, other arithmetic, local(): quotient = recorded[0] / blurred  30.1 us
    log x2, other arithmetic, local(): log_terms = jnp.log(correction)  30.1 us
    add x2, other arithmetic, local(): log_total + lax.ppermute(log_total, 'view', [(dev, dev ^ hop) for dev in...  30.1 us
    ppermute x4, waiting for transfers between devices, with_halo(): after = lax.ppermute(initial, axis, down)  25.3 us
    ppermute x4, starting transfers between devices, with_halo(): before = lax.ppermute(last, axis, up)  20.3 us
    ppermute x4, waiting for transfers between devices, with_halo(): before = lax.ppermute(last, axis, up)  9.63 us
  transfers between devices with their start and end apart: 12, of which 12 were waited for; matrix products, arithmetic and copies ran while one was open for 1% of the time, Pallas kernels for 0%

profile of v1, /device:TPU:0, one launch (start us, length us, event | category | flops | bytes accessed | tf_op | source)
XLA Modules:
  0.0 336.9 jit_solution(16275903649097213465)
XLA Ops:
  0.0 1.3 fusion.365
  1.4 5.0 %collective-permute-start = (f32[7,16,1024]{2,1,0:T(8,128)S(1)}, f32[7,16,1024]{2,1,0:T(8,128)S(1)}, u32[]{:S(2)}, u32[]{:S(2)}) collective-permute-start(f32[7,16,1024]{2,1,0:T(8,128)S(1)} %get-tuple-element.13), channel_id=1, source_target_pairs={{0,4},{4,8},{8,12},{1,5},{5,9},{9,13},{2,6},{6,10},{10,14},{3,7},{... | collective-permute-start | bytes 1376264 | tf_op jit(solution)/shard_map/ppermute | solution.py:17
  6.4 1.3 collective-permute-start.1
  7.7 0.1 reduce_sum.9
  7.8 0.1 broadcast_divide_fusion
  7.8 0.7 fusion.367
  8.6 0.7 fusion.368
  9.3 0.7 fusion.366
  10.0 6.1 %collective-permute-done = f32[7,16,1024]{2,1,0:T(8,128)S(1)} collective-permute-done((f32[7,16,1024]{2,1,0:T(8,128)S(1)}, f32[7,16,1024]{2,1,0:T(8,128)S(1)}, u32[]{:S(2)}, u32[]{:S(2)}) %collective-permute-start) | collective-permute-done | bytes 458784 | tf_op jit(solution)/shard_map/ppermute | solution.py:17
  16.1 0.4 constant_dynamic-update-slice_fusion
  16.6 3.7 %collective-permute-done.1 = f32[7,16,1024]{2,1,0:T(8,128)S(1)} collective-permute-done((f32[7,16,1024]{2,1,0:T(8,128)S(1)}, f32[7,16,1024]{2,1,0:T(8,128)S(1)}, u32[]{:S(2)}, u32[]{:S(2)}) %collective-permute-start.1) | collective-permute-done | bytes 458784 | tf_op jit(solution)/shard_map/ppermute | solution.py:18
  20.3 12.4 %fusion.346 = f32[24,16,1024]{2,1,0:T(8,128)S(1)} fusion(f32[31,16,1024]{2,1,0:T(8,128)S(1)} %constant_dynamic-update-slice_fusion.2, f32[31,16,1024]{2,1,0:T(8,128)S(1)} %get-tuple-element.11, f32[24,16,1024]{2,1,0:T(8,128)S(1)} %copy-done, f32[]{:T(128)} %bitcast.19, f32[]{:T(128)} %bitcast.18, f32[]{:T(128)} %bitcast.17, f32[]{:T(128)} %bitcast.16, ...), kind=kLoop, calls=%fused_computation.537 | loop fusion | flops 11403264 | bytes 25165884 | tf_op jit(solution)/shard_map/add | solution.py:30
  32.7 12.4 %fusion.242 = f32[24,16,1024]{2,1,0:T(8,128)S(1)} fusion(f32[24,16,1024]{2,1,0:T(8,128)S(1)} %fusion.346, f32[]{:T(128)} %bitcast.32, f32[]{:T(128)} %bitcast.31, f32[]{:T(128)} %bitcast.30, f32[]{:T(128)} %bitcast.29, f32[]{:T(128)} %bitcast.28, f32[]{:T(128)} %bitcast.27, f32[]{:T(128)} %bitcast.26, f32[]{:T(128)} %bitcast.25, f32[]{:T(128)} %bitcast.24, ...), kind=kLoop, calls=%fused_computation.426 | loop fusion | flops 11403264 | bytes 3145788 | tf_op jit(solution)/shard_map/add | solution.py:30
  45.1 15.0 %fusion.15 = f32[24,16,1024]{2,1,0:T(8,128)S(1)} fusion(f32[24,16,1024]{2,1,0:T(8,128)S(1)} %fusion.242, f32[1,24,16,1024]{3,2,1,0:T(8,128)S(1)} %copy-done.1, f32[]{:T(128)} %bitcast.45, f32[]{:T(128)} %bitcast.44, f32[]{:T(128)} %bitcast.43, f32[]{:T(128)} %bitcast.42, f32[]{:T(128)} %bitcast.41, f32[]{:T(128)} %bitcast.40, f32[]{:T(128)} %bitcast.39, ...), kind=kLoop, calls=%fused_computation.199 | loop fusion | flops 11796480 | bytes 4718652 | tf_op jit(solution)/shard_map/div | solution.py:55
  60.1 0.1 fusion.364
  60.2 1.3 collective-permute-start.3
  61.5 4.8 %collective-permute-start.2 = (f32[7,16,1024]{2,1,0:T(8,128)S(1)}, f32[7,16,1024]{2,1,0:T(8,128)S(1)}, u32[]{:S(2)}, u32[]{:S(2)}) collective-permute-start(f32[7,16,1024]{2,1,0:T(8,128)S(1)} %get-tuple-element.9), channel_id=1, source_target_pairs={{0,4},{4,8},{8,12},{1,5},{5,9},{9,13},{2,6},{6,10},{10,14},{3,7},{... | collective-permute-start | bytes 1376264 | tf_op jit(solution)/shard_map/ppermute | solution.py:17
  66.3 7.0 %collective-permute-done.3 = f32[7,16,1024]{2,1,0:T(8,128)S(1)} collective-permute-done((f32[7,16,1024]{2,1,0:T(8,128)S(1)}, f32[7,16,1024]{2,1,0:T(8,128)S(1)}, u32[]{:S(2)}, u32[]{:S(2)}) %collective-permute-start.3) | collective-permute-done | bytes 458784 | tf_op jit(solution)/shard_map/ppermute | solution.py:18
  73.3 1.2 collective-permute-done.2
  74.4 12.6 %fusion.193 = f32[24,16,1024]{2,1,0:T(8,128)S(1)} fusion(f32[24,16,1024]{2,1,0:T(8,128)S(1)} %fusion.15, f32[7,16,1024]{2,1,0:T(8,128)S(1)} %collective-permute-done.3, f32[7,16,1024]{2,1,0:T(8,128)S(1)} %collective-permute-done.2, f32[]{:T(128)} %bitcast.19, f32[]{:T(128)} %bitcast.18, f32[]{:T(128)} %bitcast.17, f32[]{:T(128)} %bitcast.16, f32[]{:T(128)} %bitcast.15, ...), kind=kLoop, calls=%fused_computation.377 | loop fusion | flops 16908288 | bytes 4063292 | tf_op jit(solution)/shard_map/add | solution.py:30
  87.0 12.3 %fusion.270 = f32[24,16,1024]{2,1,0:T(8,128)S(1)} fusion(f32[24,16,1024]{2,1,0:T(8,128)S(1)} %fusion.193, f32[]{:T(128)} %bitcast.32, f32[]{:T(128)} %bitcast.31, f32[]{:T(128)} %bitcast.30, f32[]{:T(128)} %bitcast.29, f32[]{:T(128)} %bitcast.28, f32[]{:T(128)} %bitcast.27, f32[]{:T(128)} %bitcast.26, f32[]{:T(128)} %bitcast.25, f32[]{:T(128)} %bitcast.24, ...), kind=kLoop, calls=%fused_computation.454 | loop fusion | flops 11403264 | bytes 3145788 | tf_op jit(solution)/shard_map/add | solution.py:30
  99.4 15.0 %fusion.361 = f32[24,16,1024]{2,1,0:T(8,128)S(1)} fusion(f32[24,16,1024]{2,1,0:T(8,128)S(1)} %fusion.270, f32[]{:T(128)} %bitcast.45, f32[]{:T(128)} %bitcast.44, f32[]{:T(128)} %bitcast.43, f32[]{:T(128)} %bitcast.42, f32[]{:T(128)} %bitcast.41, f32[]{:T(128)} %bitcast.40, f32[]{:T(128)} %bitcast.39, f32[]{:T(128)} %bitcast.38, f32[]{:T(128)} %bitcast.37, ...), kind=kLoop, calls=%fused_computation.567 | loop fusion | flops 11403264 | bytes 3145788 | tf_op jit(solution)/shard_map/log | solution.py:60
  114.4 0.1 collective-permute-start.4
  114.5 3.4 %collective-permute-done.4 = f32[24,16,1024]{2,1,0:T(8,128)S(1)} collective-permute-done((f32[24,16,1024]{2,1,0:T(8,128)S(1)}, f32[24,16,1024]{2,1,0:T(8,128)S(1)}, u32[]{:S(2)}, u32[]{:S(2)}) %collective-permute-start.4) | collective-permute-done | bytes 1572896 | tf_op jit(solution)/shard_map/ppermute | solution.py:63
  117.9 15.0 %fusion.370 = f32[24,16,1024]{2,1,0:T(8,128)S(1)} fusion(f32[24,16,1024]{2,1,0:T(8,128)S(1)} %collective-permute-done.4, f32[]{:T(128)} %bitcast.4, f32[]{:T(128)} %bitcast.33, f32[]{:T(128)} %bitcast.34, f32[]{:T(128)} %bitcast.35, f32[]{:T(128)} %bitcast.36, f32[]{:T(128)} %bitcast.37, f32[]{:T(128)} %bitcast.38, f32[24,16,1024]{2,1,0:T(8,128)S(1)} %fusion.270, ...), kind=kLoop, calls=%fused_computation.581 | loop fusion | flops 11796480 | bytes 4718652 | tf_op jit(solution)/shard_map/add | solution.py:63
  132.9 1.6 collective-permute-start.5
  134.5 34.9 %collective-permute-done.5 = f32[24,16,1024]{2,1,0:T(8,128)S(1)} collective-permute-done((f32[24,16,1024]{2,1,0:T(8,128)S(1)}, f32[24,16,1024]{2,1,0:T(8,128)S(1)}, u32[]{:S(2)}, u32[]{:S(2)}) %collective-permute-start.5) | collective-permute-done | bytes 1572896 | tf_op jit(solution)/shard_map/ppermute | solution.py:63
  169.4 0.5 exponential_multiply_fusion.1
  169.9 0.1 fusion.363
  170.0 1.3 collective-permute-start.7
  171.3 5.3 %collective-permute-start.6 = (f32[7,16,1024]{2,1,0:T(8,128)S(1)}, f32[7,16,1024]{2,1,0:T(8,128)S(1)}, u32[]{:S(2)}, u32[]{:S(2)}) collective-permute-start(f32[7,16,1024]{2,1,0:T(8,128)S(1)} %get-tuple-element.7), channel_id=1, source_target_pairs={{0,4},{4,8},{8,12},{1,5},{5,9},{9,13},{2,6},{6,10},{10,14},{3,7},{... | collective-permute-start | bytes 1376264 | tf_op jit(solution)/shard_map/ppermute | solution.py:17
  176.6 7.8 %collective-permute-done.7 = f32[7,16,1024]{2,1,0:T(8,128)S(1)} collective-permute-done((f32[7,16,1024]{2,1,0:T(8,128)S(1)}, f32[7,16,1024]{2,1,0:T(8,128)S(1)}, u32[]{:S(2)}, u32[]{:S(2)}) %collective-permute-start.7) | collective-permute-done | bytes 458784 | tf_op jit(solution)/shard_map/ppermute | solution.py:18
  184.4 1.2 collective-permute-done.6
  185.5 12.6 %fusion.155 = f32[24,16,1024]{2,1,0:T(8,128)S(1)} fusion(f32[24,16,1024]{2,1,0:T(8,128)S(1)} %exponential_multiply_fusion.1, f32[7,16,1024]{2,1,0:T(8,128)S(1)} %collective-permute-done.7, f32[7,16,1024]{2,1,0:T(8,128)S(1)} %collective-permute-done.6, f32[]{:T(128)} %bitcast.19, f32[]{:T(128)} %bitcast.18, f32[]{:T(128)} %bitcast.17, f32[]{:T(128)} %bitcast.16, ...), kind=kLoop, calls=%fused_computation.339 | loop fusion | flops 16908288 | bytes 4063292 | tf_op jit(solution)/shard_map/add | solution.py:30
  198.1 12.3 %fusion.298 = f32[24,16,1024]{2,1,0:T(8,128)S(1)} fusion(f32[24,16,1024]{2,1,0:T(8,128)S(1)} %fusion.155, f32[]{:T(128)} %bitcast.32, f32[]{:T(128)} %bitcast.31, f32[]{:T(128)} %bitcast.30, f32[]{:T(128)} %bitcast.29, f32[]{:T(128)} %bitcast.28, f32[]{:T(128)} %bitcast.27, f32[]{:T(128)} %bitcast.26, f32[]{:T(128)} %bitcast.25, f32[]{:T(128)} %bitcast.24, ...), kind=kLoop, calls=%fused_computation.482 | loop fusion | flops 11403264 | bytes 3145788 | tf_op jit(solution)/shard_map/add | solution.py:30
  210.5 15.0 %fusion.72 = f32[24,16,1024]{2,1,0:T(8,128)S(1)} fusion(f32[24,16,1024]{2,1,0:T(8,128)S(1)} %fusion.298, f32[1,24,16,1024]{3,2,1,0:T(8,128)S(1)} %copy-done.1, f32[]{:T(128)} %bitcast.45, f32[]{:T(128)} %bitcast.44, f32[]{:T(128)} %bitcast.43, f32[]{:T(128)} %bitcast.42, f32[]{:T(128)} %bitcast.41, f32[]{:T(128)} %bitcast.40, f32[]{:T(128)} %bitcast.39, ...), kind=kLoop, calls=%fused_computation.256 | loop fusion | flops 11796480 | bytes 4718652 | tf_op jit(solution)/shard_map/div | solution.py:55
  225.6 1.3 collective-permute-start.9
  226.9 5.3 %collective-permute-start.8 = (f32[7,16,1024]{2,1,0:T(8,128)S(1)}, f32[7,16,1024]{2,1,0:T(8,128)S(1)}, u32[]{:S(2)}, u32[]{:S(2)}) collective-permute-start(f32[7,16,1024]{2,1,0:T(8,128)S(1)} %get-tuple-element.5), channel_id=1, source_target_pairs={{0,4},{4,8},{8,12},{1,5},{5,9},{9,13},{2,6},{6,10},{10,14},{3,7},{... | collective-permute-start | bytes 1376264 | tf_op jit(solution)/shard_map/ppermute | solution.py:17
  232.2 6.9 %collective-permute-done.9 = f32[7,16,1024]{2,1,0:T(8,128)S(1)} collective-permute-done((f32[7,16,1024]{2,1,0:T(8,128)S(1)}, f32[7,16,1024]{2,1,0:T(8,128)S(1)}, u32[]{:S(2)}, u32[]{:S(2)}) %collective-permute-start.9) | collective-permute-done | bytes 458784 | tf_op jit(solution)/shard_map/ppermute | solution.py:18
  239.1 1.2 collective-permute-done.8
  240.2 12.6 %fusion.117 = f32[24,16,1024]{2,1,0:T(8,128)S(1)} fusion(f32[24,16,1024]{2,1,0:T(8,128)S(1)} %fusion.72, f32[7,16,1024]{2,1,0:T(8,128)S(1)} %collective-permute-done.9, f32[7,16,1024]{2,1,0:T(8,128)S(1)} %collective-permute-done.8, f32[]{:T(128)} %bitcast.19, f32[]{:T(128)} %bitcast.18, f32[]{:T(128)} %bitcast.17, f32[]{:T(128)} %bitcast.16, f32[]{:T(128)} %bitcast.15, ...), kind=kLoop, calls=%fused_computation.301 | loop fusion | flops 16908288 | bytes 4063292 | tf_op jit(solution)/shard_map/add | solution.py:30
  252.9 12.3 %fusion.326 = f32[24,16,1024]{2,1,0:T(8,128)S(1)} fusion(f32[24,16,1024]{2,1,0:T(8,128)S(1)} %fusion.117, f32[]{:T(128)} %bitcast.32, f32[]{:T(128)} %bitcast.31, f32[]{:T(128)} %bitcast.30, f32[]{:T(128)} %bitcast.29, f32[]{:T(128)} %bitcast.28, f32[]{:T(128)} %bitcast.27, f32[]{:T(128)} %bitcast.26, f32[]{:T(128)} %bitcast.25, f32[]{:T(128)} %bitcast.24, ...), kind=kLoop, calls=%fused_computation.510 | loop fusion | flops 11403264 | bytes 3145788 | tf_op jit(solution)/shard_map/add | solution.py:30
  265.2 15.0 %fusion.360 = f32[24,16,1024]{2,1,0:T(8,128)S(1)} fusion(f32[24,16,1024]{2,1,0:T(8,128)S(1)} %fusion.326, f32[]{:T(128)} %bitcast.45, f32[]{:T(128)} %bitcast.44, f32[]{:T(128)} %bitcast.43, f32[]{:T(128)} %bitcast.42, f32[]{:T(128)} %bitcast.41, f32[]{:T(128)} %bitcast.40, f32[]{:T(128)} %bitcast.39, f32[]{:T(128)} %bitcast.38, f32[]{:T(128)} %bitcast.37, ...), kind=kLoop, calls=%fused_computation.566 | loop fusion | flops 11403264 | bytes 3145788 | tf_op jit(solution)/shard_map/log | solution.py:60
  280.3 3.4 %collective-permute-done.10 = f32[24,16,1024]{2,1,0:T(8,128)S(1)} collective-permute-done((f32[24,16,1024]{2,1,0:T(8,128)S(1)}, f32[24,16,1024]{2,1,0:T(8,128)S(1)}, u32[]{:S(2)}, u32[]{:S(2)}) %collective-permute-start.10) | collective-permute-done | bytes 1572896 | tf_op jit(solution)/shard_map/ppermute | solution.py:63
  283.7 15.0 %fusion.369 = f32[24,16,1024]{2,1,0:T(8,128)S(1)} fusion(f32[24,16,1024]{2,1,0:T(8,128)S(1)} %collective-permute-done.10, f32[]{:T(128)} %bitcast.4, f32[]{:T(128)} %bitcast.33, f32[]{:T(128)} %bitcast.34, f32[]{:T(128)} %bitcast.35, f32[]{:T(128)} %bitcast.36, f32[]{:T(128)} %bitcast.37, f32[]{:T(128)} %bitcast.38, f32[24,16,1024]{2,1,0:T(8,128)S(1)} %fusion.326, ...), kind=kLoop, calls=%fused_computation.580 | loop fusion | flops 11796480 | bytes 4718652 | tf_op jit(solution)/shard_map/add | solution.py:63
  298.7 1.6 collective-permute-start.11
  300.3 34.9 %collective-permute-done.11 = f32[24,16,1024]{2,1,0:T(8,128)S(1)} collective-permute-done((f32[24,16,1024]{2,1,0:T(8,128)S(1)}, f32[24,16,1024]{2,1,0:T(8,128)S(1)}, u32[]{:S(2)}, u32[]{:S(2)}) %collective-permute-start.11) | collective-permute-done | bytes 1572896 | tf_op jit(solution)/shard_map/ppermute | solution.py:63
  335.2 1.6 exponential_multiply_fusion
  (10 shorter events, 0.2 us)
Async XLA Ops:
  0.0 16.1 %copy-start = (f32[24,16,1024]{2,1,0:T(8,128)S(1)}, f32[24,16,1024]{2,1,0:T(8,128)}, u32[]{:S(2)}) copy-start(f32[24,16,1024]{2,1,0:T(8,128)} %param.5) | copy-start | bytes 4718596
  0.0 7.7 %copy-start.2 = (f32[1,3,15]{2,0,1:T(1,128)S(1)}, f32[1,3,15]{2,0,1:T(1,128)}, u32[]{:S(2)}) copy-start(f32[1,3,15]{2,0,1:T(1,128)} %param.4) | copy-start | bytes 544
  1.4 14.7 %collective-permute-start = (f32[7,16,1024]{2,1,0:T(8,128)S(1)}, f32[7,16,1024]{2,1,0:T(8,128)S(1)}, u32[]{:S(2)}, u32[]{:S(2)}) collective-permute-start(f32[7,16,1024]{2,1,0:T(8,128)S(1)} %get-tuple-element.13), channel_id=1, source_target_pairs={{0,4},{4,8},{8,12},{1,5},{5,9},{9,13},{2,6},{6,10},{10,14},{3,7},{... | collective-permute-start | bytes 1376264 | tf_op jit(solution)/shard_map/ppermute | solution.py:17
  6.4 13.9 %collective-permute-start.1 = (f32[7,16,1024]{2,1,0:T(8,128)S(1)}, f32[7,16,1024]{2,1,0:T(8,128)S(1)}, u32[]{:S(2)}, u32[]{:S(2)}) collective-permute-start(f32[7,16,1024]{2,1,0:T(8,128)S(1)} %get-tuple-element.14), channel_id=1, source_target_pairs={{4,0},{8,4},{12,8},{5,1},{9,5},{13,9},{6,2},{10,6},{14,10},{7,3},{... | collective-permute-start | bytes 1376264 | tf_op jit(solution)/shard_map/ppermute | solution.py:18
  32.6 12.4 %copy-start.1 = (f32[1,24,16,1024]{3,2,1,0:T(8,128)S(1)}, f32[1,24,16,1024]{3,2,1,0:T(8,128)}, u32[]{:S(2)}) copy-start(f32[1,24,16,1024]{3,2,1,0:T(8,128)} %param.3) | copy-start | bytes 4718596
  60.2 13.0 %collective-permute-start.3 = (f32[7,16,1024]{2,1,0:T(8,128)S(1)}, f32[7,16,1024]{2,1,0:T(8,128)S(1)}, u32[]{:S(2)}, u32[]{:S(2)}) collective-permute-start(f32[7,16,1024]{2,1,0:T(8,128)S(1)} %get-tuple-element.10), channel_id=1, source_target_pairs={{4,0},{8,4},{12,8},{5,1},{9,5},{13,9},{6,2},{10,6},{14,10},{7,3},{... | collective-permute-start | bytes 1376264 | tf_op jit(solution)/shard_map/ppermute | solution.py:18
  61.5 12.9 %collective-permute-start.2 = (f32[7,16,1024]{2,1,0:T(8,128)S(1)}, f32[7,16,1024]{2,1,0:T(8,128)S(1)}, u32[]{:S(2)}, u32[]{:S(2)}) collective-permute-start(f32[7,16,1024]{2,1,0:T(8,128)S(1)} %get-tuple-element.9), channel_id=1, source_target_pairs={{0,4},{4,8},{8,12},{1,5},{5,9},{9,13},{2,6},{6,10},{10,14},{3,7},{... | collective-permute-start | bytes 1376264 | tf_op jit(solution)/shard_map/ppermute | solution.py:17
  114.4 3.5 %collective-permute-start.4 = (f32[24,16,1024]{2,1,0:T(8,128)S(1)}, f32[24,16,1024]{2,1,0:T(8,128)S(1)}, u32[]{:S(2)}, u32[]{:S(2)}) collective-permute-start(f32[24,16,1024]{2,1,0:T(8,128)S(1)} %fusion.361), channel_id=1, source_target_pairs={{0,1},{1,0},{2,3},{3,2},{4,5},{5,4},{6,7},{7,6},{8,9},{9,8},{10,11... | collective-permute-start | bytes 4718600 | tf_op jit(solution)/shard_map/ppermute | solution.py:63
  132.9 36.5 %collective-permute-start.5 = (f32[24,16,1024]{2,1,0:T(8,128)S(1)}, f32[24,16,1024]{2,1,0:T(8,128)S(1)}, u32[]{:S(2)}, u32[]{:S(2)}) collective-permute-start(f32[24,16,1024]{2,1,0:T(8,128)S(1)} %fusion.370), channel_id=1, source_target_pairs={{0,2},{1,3},{2,0},{3,1},{4,6},{5,7},{6,4},{7,5},{8,10},{9,11},{10,... | collective-permute-start | bytes 4718600 | tf_op jit(solution)/shard_map/ppermute | solution.py:63
  170.0 14.3 %collective-permute-start.7 = (f32[7,16,1024]{2,1,0:T(8,128)S(1)}, f32[7,16,1024]{2,1,0:T(8,128)S(1)}, u32[]{:S(2)}, u32[]{:S(2)}) collective-permute-start(f32[7,16,1024]{2,1,0:T(8,128)S(1)} %get-tuple-element.8), channel_id=1, source_target_pairs={{4,0},{8,4},{12,8},{5,1},{9,5},{13,9},{6,2},{10,6},{14,10},{7,3},{... | collective-permute-start | bytes 1376264 | tf_op jit(solution)/shard_map/ppermute | solution.py:18
  171.3 14.2 %collective-permute-start.6 = (f32[7,16,1024]{2,1,0:T(8,128)S(1)}, f32[7,16,1024]{2,1,0:T(8,128)S(1)}, u32[]{:S(2)}, u32[]{:S(2)}) collective-permute-start(f32[7,16,1024]{2,1,0:T(8,128)S(1)} %get-tuple-element.7), channel_id=1, source_target_pairs={{0,4},{4,8},{8,12},{1,5},{5,9},{9,13},{2,6},{6,10},{10,14},{3,7},{... | collective-permute-start | bytes 1376264 | tf_op jit(solution)/shard_map/ppermute | solution.py:17
  225.6 13.5 %collective-permute-start.9 = (f32[7,16,1024]{2,1,0:T(8,128)S(1)}, f32[7,16,1024]{2,1,0:T(8,128)S(1)}, u32[]{:S(2)}, u32[]{:S(2)}) collective-permute-start(f32[7,16,1024]{2,1,0:T(8,128)S(1)} %get-tuple-element.6), channel_id=1, source_target_pairs={{4,0},{8,4},{12,8},{5,1},{9,5},{13,9},{6,2},{10,6},{14,10},{7,3},{... | collective-permute-start | bytes 1376264 | tf_op jit(solution)/shard_map/ppermute | solution.py:18
  226.9 13.4 %collective-permute-start.8 = (f32[7,16,1024]{2,1,0:T(8,128)S(1)}, f32[7,16,1024]{2,1,0:T(8,128)S(1)}, u32[]{:S(2)}, u32[]{:S(2)}) collective-permute-start(f32[7,16,1024]{2,1,0:T(8,128)S(1)} %get-tuple-element.5), channel_id=1, source_target_pairs={{0,4},{4,8},{8,12},{1,5},{5,9},{9,13},{2,6},{6,10},{10,14},{3,7},{... | collective-permute-start | bytes 1376264 | tf_op jit(solution)/shard_map/ppermute | solution.py:17
  280.2 3.5 %collective-permute-start.10 = (f32[24,16,1024]{2,1,0:T(8,128)S(1)}, f32[24,16,1024]{2,1,0:T(8,128)S(1)}, u32[]{:S(2)}, u32[]{:S(2)}) collective-permute-start(f32[24,16,1024]{2,1,0:T(8,128)S(1)} %fusion.360), channel_id=1, source_target_pairs={{0,1},{1,0},{2,3},{3,2},{4,5},{5,4},{6,7},{7,6},{8,9},{9,8},{10,11... | collective-permute-start | bytes 4718600 | tf_op jit(solution)/shard_map/ppermute | solution.py:63
  298.7 36.5 %collective-permute-start.11 = (f32[24,16,1024]{2,1,0:T(8,128)S(1)}, f32[24,16,1024]{2,1,0:T(8,128)S(1)}, u32[]{:S(2)}, u32[]{:S(2)}) collective-permute-start(f32[24,16,1024]{2,1,0:T(8,128)S(1)} %fusion.369), channel_id=1, source_target_pairs={{0,2},{1,3},{2,0},{3,1},{4,6},{5,7},{6,4},{7,5},{8,10},{9,11},{10,... | collective-permute-start | bytes 4718600 | tf_op jit(solution)/shard_map/ppermute | solution.py:63
